TPU v7x, 32 devices: a whole 2x2x4 slice. The times are simulated.
32 devices in a mesh: stn: 8 (over z, core), win: 4 (over y, x).
Axes of the slice: x: 2, y: 2, z: 4, core: 2. Of those that a mesh axis runs over, the one named last changes fastest.
Arguments:
- records: bfloat16 [128, 4, 3, 8192], P('stn', 'win'), may hold values from -6 to 6
- observed: float32 [128, 3, 3, 256], P('stn'), may hold values from -6 to 6
- lag_lo: int32 [128], P('stn'), may hold values from 0 to 63
- lag_hi: int32 [128], P('stn'), may hold values from 192 to 256
- send_table: int32 [8, 8, 1], P('stn'), may hold values from 0 to 15, as said below
- pair_first: int32 [128], P('stn'), may hold values from 0 to 7, as said below
- pair_second: int32 [128], P('stn'), may hold values from 0 to 7, as said below
Outputs:
- station_adjoint: bfloat16 [128, 4, 3, 8192], P('stn', 'win')
- residual: float32 [128, 3, 3, 256], P(('stn', 'win'))
Inputs may be any that keep to these rules, and one draw needn't show every extreme that they name: Each entry send_table[g, o, :] names 1 different local stations of group g. `pair_first`: slot indices at the pair's owner; a pair's two slots differ, no two pairs of an owner join the same two slots, and every slot of an owner is named by some pair. `pair_second`: slot indices at the pair's owner, as for pair_first.
All inputs are finite; a program needn't handle non-finite values.
Results may differ from a plain program's by a relative error of at most 0.0053.
Values may be sent and summed in bfloat16 or wider, within the bound.
No kernel may reach another device: no remote copies, remote signals or barrier semaphores. Data moves between devices by JAX's collectives and lax.ppermute only.
A program may use at most 192 MiB of HBM per device.

v0:
```python
import math
import jax
import jax.numpy as jnp
from jax import lax
from jax.sharding import PartitionSpec as P

LAGS = 256


def forward_table(lag_count):
    period = 2 * lag_count
    sample_ids = jnp.arange(lag_count, dtype=jnp.int32)
    freq_ids = jnp.arange(lag_count, dtype=jnp.int32)
    phase = (sample_ids[:, None] * freq_ids[None, :] % period).astype(jnp.float32) * (
        math.pi / lag_count
    )
    parity = (1 - 2 * (sample_ids % 2)).astype(jnp.float32)
    cosines = jnp.cos(phase)
    sines = jnp.where(freq_ids[None, :] == 0, parity[:, None], jnp.sin(phase))
    return jnp.concatenate([cosines, sines], axis=1)


def inverse_rows(positions, sine_sign, lag_count):
    period = 2 * lag_count
    freq_ids = jnp.arange(lag_count, dtype=jnp.int32)
    wrapped = positions % period
    phase = (freq_ids[:, None] * wrapped[None, :] % period).astype(jnp.float32) * (
        math.pi / lag_count
    )
    weight = jnp.where(freq_ids == 0, 1.0 / period, 2.0 / period).astype(jnp.float32)
    cos_rows = weight[:, None] * jnp.cos(phase)
    parity = (1 - 2 * (wrapped % 2)).astype(jnp.float32) / period
    sin_rows = jnp.where(
        freq_ids[:, None] == 0, parity[None, :], sine_sign * (2.0 / period) * jnp.sin(phase)
    )
    return jnp.concatenate([cos_rows, sin_rows], axis=0)


def shards(records, observed, lag_lo, lag_hi, send_table, pair_first, pair_second):
    owner_count = lax.axis_size("stn")
    window_groups = lax.axis_size("win")
    send_rows = send_table[0]
    cap_count = send_rows.shape[1]
    slot_count = owner_count * cap_count
    local_windows = records.shape[1]
    samples = records.shape[3]
    station_count = records.shape[0]
    lag_count = LAGS
    half_lag = lag_count // 2
    block_total = samples // lag_count
    highest = lax.Precision.HIGHEST
    outgoing = jnp.take(records, send_rows.reshape(-1), axis=0)
    outgoing = outgoing.reshape((owner_count, cap_count) + records.shape[1:])
    arrived = lax.all_to_all(outgoing, "stn", split_axis=0, concat_axis=0, tiled=True)
    slot_records = arrived.reshape((slot_count,) + records.shape[1:])
    spectral = forward_table(lag_count)
    lag_ids = jnp.arange(lag_count, dtype=jnp.int32)
    corr_table = inverse_rows(lag_ids, -1.0, lag_count)
    middle_table = inverse_rows(lag_ids + half_lag, 1.0, lag_count)
    lower_table = (
        inverse_rows(lag_ids + 3 * half_lag, 1.0, lag_count)
        * (lag_ids < half_lag).astype(jnp.float32)[None, :]
    )
    upper_table = (
        inverse_rows(lag_ids - half_lag, 1.0, lag_count)
        * (lag_ids >= half_lag).astype(jnp.float32)[None, :]
    )
    column_ids = jnp.arange(2 * lag_count, dtype=jnp.int32)
    shift_sign = (1 - 2 * (column_ids % lag_count % 2)).astype(jnp.float32)
    first_col = (lag_ids == 0).astype(jnp.float32)
    other_cols = 1.0 - first_col
    block_shape = (slot_count, local_windows, 3, block_total, lag_count)
    first_blocks = slot_records.astype(jnp.float32).reshape(block_shape)
    x_spec = jnp.dot(first_blocks, spectral, precision=highest)
    shifted = jnp.pad(slot_records, ((0, 0), (0, 0), (0, 0), (half_lag, lag_count - half_lag)))
    shifted = shifted.astype(jnp.float32).reshape(
        (slot_count, local_windows, 3, block_total + 1, lag_count)
    )
    z_spec = jnp.dot(shifted, spectral, precision=highest)
    y_spec = z_spec[..., :-1, :] + shift_sign * z_spec[..., 1:, :]
    slot_ids = jnp.arange(slot_count, dtype=jnp.int32)
    first_hot = (pair_first[:, None] == slot_ids[None, :]).astype(jnp.float32)
    second_hot = (pair_second[:, None] == slot_ids[None, :]).astype(jnp.float32)
    x_pair = jnp.einsum("ps,swakf->pwakf", first_hot, x_spec, precision=highest)
    y_pair = jnp.einsum("ps,swakf->pwakf", second_hot, y_spec, precision=highest)
    x_cos = x_pair[..., :lag_count]
    x_sin = x_pair[..., lag_count:]
    y_cos = y_pair[..., :lag_count]
    y_sin = y_pair[..., lag_count:]
    y_sin_other = y_sin * other_cols
    y_mixed = y_sin * first_col + y_cos * other_cols

    def cross_terms(left, right):
        return jnp.einsum("pwakf,pwbkf->pabf", left, right, precision=highest)

    real_part = cross_terms(x_cos, y_cos) + cross_terms(x_sin, y_sin_other)
    imag_part = cross_terms(x_sin, y_mixed) - cross_terms(x_cos, y_sin_other)
    cross = jnp.concatenate([real_part, imag_part], axis=-1)
    partial_corr = jnp.dot(cross, corr_table, precision=highest)
    pair_count = partial_corr.shape[0]
    corr_scale = 1.0 / math.sqrt(samples * local_windows * window_groups)
    lag_mask = (lag_ids[None, :] >= lag_lo[:, None]) & (lag_ids[None, :] < lag_hi[:, None])
    share_rows = pair_count // window_groups
    offset = lax.axis_index("win") * share_rows
    summed = lax.psum(partial_corr, "win")
    residual_all = jnp.where(lag_mask[:, None, None, :], summed * corr_scale - observed, 0.0)
    adjoint_source = residual_all.astype(jnp.bfloat16)
    residual_share = lax.dynamic_slice_in_dim(residual_all, offset, share_rows, 0)
    source_spec = jnp.dot(adjoint_source.astype(jnp.float32), spectral, precision=highest)
    src_cos = source_spec[..., :lag_count]
    src_sin = source_spec[..., lag_count:]
    src_cos_other = src_cos * other_cols
    src_sin_other = src_sin * other_cols
    src_sin_first = src_sin * first_col

    def first_terms(source, data):
        return jnp.einsum("pabf,pwbkf->pwakf", source, data, precision=highest)

    first_real = first_terms(src_cos, y_cos) + first_terms(src_sin_other, y_sin)
    first_imag = first_terms(src_sin, y_mixed) - first_terms(src_cos_other, y_sin)
    first_pair = jnp.concatenate([first_real, first_imag], axis=-1)
    first_acc = jnp.einsum("ps,pwakf->swakf", first_hot, first_pair, precision=highest)

    def second_terms(data, source):
        return jnp.einsum("pwakf,pabf->pwbkf", data, source, precision=highest)

    second_real = second_terms(x_cos, src_cos) - second_terms(x_sin, src_sin_other)
    second_imag = (
        second_terms(x_cos, src_sin_other)
        + second_terms(x_sin, src_cos_other)
        + second_terms(x_sin, src_sin_first)
    )
    second_pair = jnp.concatenate([second_real, second_imag], axis=-1)
    second_acc = jnp.einsum("ps,pwakf->swakf", second_hot, second_pair, precision=highest)
    first_time = jnp.dot(first_acc, corr_table, precision=highest)
    middle = jnp.dot(second_acc, middle_table, precision=highest)
    from_lower = jnp.dot(second_acc, lower_table, precision=highest)
    from_upper = jnp.dot(second_acc, upper_table, precision=highest)
    spacer = ((0, 0), (0, 0), (0, 0))
    from_lower = jnp.pad(from_lower[..., :-1, :], spacer + ((1, 0), (0, 0)))
    from_upper = jnp.pad(from_upper[..., 1:, :], spacer + ((0, 1), (0, 0)))
    slot_sum = (first_time + middle + from_lower + from_upper).reshape(
        (slot_count,) + records.shape[1:]
    )
    adj_scale = 1.0 / math.sqrt(3 * lag_count)
    slot_adjoint = (slot_sum * adj_scale).astype(jnp.bfloat16)
    slot_adjoint = slot_adjoint.reshape((owner_count, cap_count) + records.shape[1:])
    station_ids = jnp.arange(station_count, dtype=jnp.int32)
    station_hot = (send_rows.reshape(-1)[None, :] == station_ids[:, None]).astype(jnp.bfloat16)
    returned = lax.all_to_all(slot_adjoint, "stn", split_axis=0, concat_axis=0, tiled=True)
    flat_rows = returned.reshape((slot_count, -1))
    totals = jnp.dot(station_hot, flat_rows, preferred_element_type=jnp.float32)
    station_adjoint = totals.reshape((station_count,) + returned.shape[2:]).astype(jnp.bfloat16)
    return (station_adjoint, residual_share)


def solution(mesh):
    placed = (
        P("stn", "win", None, None),
        P("stn", None, None, None),
        P("stn"),
        P("stn"),
        P("stn", None, None),
        P("stn"),
        P("stn"),
    )
    return jax.shard_map(
        shards,
        mesh=mesh,
        in_specs=placed,
        out_specs=(P("stn", "win", None, None), P(("stn", "win"), None, None, None)),
        check_vma=False,
    )
```

profile of v0, /device:TPU:0, one launch (start us, length us, event | category | flops | bytes accessed | tf_op | source)
XLA Modules:
  0.0 665.9 jit_solution(7594870986401893331)
XLA Ops:
  12.4 6.3 all-to-all-start
  20.7 6.3 cosine_multiply_fusion.2
  27.0 7.1 %all-to-all-done = bf16[8,1,1,3,8192]{4,3,2,1,0:T(4,128)(2,1)S(1)} async-done(((bf16[8,1,1,3,8192]{4,3,2,1,0:T(4,128)(2,1)}), bf16[8,1,1,3,8192]{4,3,2,1,0:T(4,128)(2,1)S(1)}, u32[]{:S(2)}, u32[]{:S(2)}) %all-to-all-start) | async-done | bytes 393248 | tf_op jit(solution)/shard_map/all_to_all | solution.py:54
  41.2 6.1 copy.158
  52.3 6.2 copy.157
  58.5 6.1 copy.156
  64.6 6.1 copy.155
  70.7 30.7 %fusion.150 = f32[16,256,3,3]{3,2,1,0:T(4,128)S(1)} fusion(f32[16,3,32,256]{2,1,3,0:T(4,128)} %copy.158, f32[16,3,32,256]{2,1,3,0:T(4,128)} %copy.157), kind=kOutput, calls=%fused_computation.225 | convolution fusion | flops 14155776 | bytes 3293184 | tf_op jit(solution)/shard_map/pwakf,pwbkf->pabf/dot_general | solution.py:94
  101.4 29.8 %subtract_bitcast_fusion.2 = f32[16,3,3,256]{1,2,3,0:T(4,128)} fusion(f32[16,256,3,3]{3,2,1,0:T(4,128)S(1)} %fusion.150, f32[16,3,32,256]{2,1,3,0:T(4,128)S(1)} %copy-done.1, f32[16,3,32,256]{2,1,3,0:T(4,128)S(1)} %copy-done), kind=kOutput, calls=%fused_computation.9 | convolution fusion | flops 14192640 | bytes 3440640 | tf_op jit(solution)/shard_map/pwakf,pwbkf->pabf/dot_general | solution.py:94
  131.2 4.9 copy.163
  136.2 6.1 copy.164
  142.3 30.4 %fusion.149 = f32[16,256,3,3]{3,2,1,0:T(4,128)S(1)} fusion(f32[16,3,32,256]{2,1,3,0:T(4,128)} %copy.164, f32[16,3,32,256]{2,1,3,0:T(4,128)} %copy.155), kind=kOutput, calls=%fused_computation.224 | convolution fusion | flops 14155776 | bytes 3293184 | tf_op jit(solution)/shard_map/pwakf,pwbkf->pabf/dot_general | solution.py:94
  172.7 31.9 %add_bitcast_fusion.2 = f32[16,3,3,256]{1,2,3,0:T(4,128)} fusion(f32[16,256,3,3]{3,2,1,0:T(4,128)S(1)} %fusion.149, f32[16,3,32,256]{2,1,3,0:T(4,128)} %copy.156, f32[16,3,32,256]{2,1,3,0:T(4,128)} %copy.157), kind=kOutput, calls=%fused_computation.10 | convolution fusion | flops 14192640 | bytes 3440640 | tf_op jit(solution)/shard_map/pwakf,pwbkf->pabf/dot_general | solution.py:94
  204.6 5.0 copy.162
  211.8 4.7 copy.166
  216.6 35.3 %all-reduce.5.cloned.1.call-done = f32[16,3,3,256]{3,0,2,1:T(8,128)} async-done(((f32[16,3,3,256]{3,0,2,1:T(8,128)}), f32[16,3,3,256]{3,0,2,1:T(8,128)}) %all-reduce.5.cloned.1.call-update) | async-done | bytes 147472 | tf_op jit(solution)/shard_map/psum | solution.py:105
  253.5 4.7 copy.174
  258.2 37.4 %fusion.151 = f32[16,256,32,3]{2,3,1,0:T(4,128)} fusion(f32[16,3,32,256]{2,1,3,0:T(4,128)} %copy.164, f32[16,3,3,256]{1,2,3,0:T(4,128)} %copy.174), kind=kOutput, calls=%fused_computation.226 | convolution fusion | flops 14155776 | bytes 3293184 | tf_op jit(solution)/shard_map/pabf,pwbkf->pwakf/dot_general | solution.py:117
  295.6 30.2 %fusion.153 = f32[16,256,3,32]{3,2,1,0:T(4,128)} fusion(f32[16,3,3,256]{1,2,3,0:T(4,128)S(1)} %copy-done.3, f32[16,3,32,256]{2,1,3,0:T(4,128)} %copy.155), kind=kOutput, calls=%fused_computation.228 | convolution fusion | flops 14155776 | bytes 3293184 | tf_op jit(solution)/shard_map/pwakf,pabf->pwbkf/dot_general | solution.py:125
  330.4 32.4 %fusion.152 = f32[16,256,32,3]{2,3,1,0:T(4,128)} fusion(f32[16,3,32,256]{2,1,3,0:T(4,128)} %copy.158, f32[16,3,3,256]{2,1,3,0:T(4,128)} %copy.169), kind=kOutput, calls=%fused_computation.227 | convolution fusion | flops 14155776 | bytes 3293184 | tf_op jit(solution)/shard_map/pabf,pwbkf->pwakf/dot_general | solution.py:117
  362.8 4.7 copy.180
  372.1 31.0 %fusion.154 = f32[16,256,3,32]{3,2,1,0:T(4,128)} fusion(f32[16,3,3,256]{1,2,3,0:T(4,128)} %copy.176, f32[16,3,32,256]{2,1,3,0:T(4,128)} %copy.155), kind=kOutput, calls=%fused_computation.229 | convolution fusion | flops 14155776 | bytes 3293184 | tf_op jit(solution)/shard_map/pwakf,pabf->pwbkf/dot_general | solution.py:125
  403.1 30.8 %fusion.155 = f32[16,256,3,32]{3,2,1,0:T(4,128)} fusion(f32[16,3,3,256]{1,2,3,0:T(4,128)S(1)} %copy-done.2, f32[16,3,32,256]{2,1,3,0:T(4,128)} %copy.157), kind=kOutput, calls=%fused_computation.230 | convolution fusion | flops 14155776 | bytes 3293184 | tf_op jit(solution)/shard_map/pwakf,pabf->pwbkf/dot_general | solution.py:125
  433.9 36.6 %subtract_bitcast_fusion.1 = f32[16,1,3,32,256]{3,2,4,0,1:T(4,128)} fusion(f32[16,256,32,3]{2,3,1,0:T(4,128)} %fusion.152, f32[16,3,32,256]{2,1,3,0:T(4,128)S(1)} %bitcast.169, f32[16,3,3,256]{1,2,3,0:T(4,128)S(1)} %copy-done.2), kind=kOutput, calls=%fused_computation.7 | convolution fusion | flops 14548992 | bytes 4866048 | tf_op jit(solution)/shard_map/pabf,pwbkf->pwakf/dot_general | solution.py:117
  470.6 36.0 %add_bitcast_fusion.1 = f32[16,1,3,32,256]{3,2,4,0,1:T(4,128)} fusion(f32[16,256,32,3]{2,3,1,0:T(4,128)S(1)} %bitcast.171, f32[16,3,32,256]{2,1,3,0:T(4,128)S(1)} %bitcast.169, f32[16,3,3,256]{1,2,3,0:T(4,128)S(1)} %bitcast.167), kind=kOutput, calls=%fused_computation.8 | convolution fusion | flops 14548992 | bytes 4866048 | tf_op jit(solution)/shard_map/pabf,pwbkf->pwakf/dot_general | solution.py:117
  506.5 12.0 %maximum_bitcast_fusion = f32[16,3,32,512]{2,1,3,0:T(4,128)} fusion(f32[16,1,3,32,256]{3,2,4,0,1:T(4,128)S(1)} %copy-done.5, f32[16,1,3,32,256]{3,2,4,0,1:T(4,128)} %add_bitcast_fusion.1), kind=kLoop, calls=%fused_computation.1 | loop fusion | flops 786432 | bytes 6291456 | tf_op jit(solution)/shard_map/reshape.43
  518.5 9.5 %copy.172 = f32[16,3,32,512]{3,0,2,1:T(8,128)S(1)} copy(f32[16,3,32,512]{2,1,3,0:T(4,128)} %maximum_bitcast_fusion) | data formatting | bytes 6291456 | tf_op jit(solution)/shard_map/reshape.43
  538.6 31.8 %subtract_bitcast_fusion = f32[16,1,3,32,256]{3,2,4,0,1:T(4,128)} fusion(f32[16,256,3,32]{3,2,1,0:T(4,128)} %fusion.153, f32[16,3,3,256]{1,2,3,0:T(4,128)} %copy.176, f32[16,3,32,256]{2,1,3,0:T(4,128)} %copy.157), kind=kOutput, calls=%fused_computation.6 | convolution fusion | flops 14548992 | bytes 4866048 | tf_op jit(solution)/shard_map/pwakf,pabf->pwbkf/dot_general | solution.py:125
  570.4 31.8 %add_bitcast_fusion = f32[16,1,3,32,256]{3,2,4,0,1:T(4,128)} fusion(f32[16,256,3,32]{3,2,1,0:T(4,128)} %fusion.154, f32[16,256,3,32]{3,2,1,0:T(4,128)} %fusion.155, f32[16,3,3,256]{1,2,3,0:T(4,128)S(1)} %copy-done.4, f32[16,3,32,256]{2,1,3,0:T(4,128)} %copy.157), kind=kOutput, calls=%fused_computation.5 | convolution fusion | flops 14942208 | bytes 6438912 | tf_op jit(solution)/shard_map/pwakf,pabf->pwbkf/dot_general | solution.py:125
  602.2 15.0 %maximum_bitcast_fusion.1 = f32[16,3,32,512]{2,1,3,0:T(4,128)} fusion(f32[16,1,3,32,256]{3,2,4,0,1:T(4,128)} %add_bitcast_fusion, f32[16,1,3,32,256]{3,2,4,0,1:T(4,128)} %subtract_bitcast_fusion), kind=kLoop, calls=%fused_computation.2 | loop fusion | flops 786432 | bytes 6291456 | tf_op jit(solution)/shard_map/reshape.57
  617.2 9.8 %copy.184 = f32[16,3,32,512]{3,0,2,1:T(8,128)S(1)} copy(f32[16,3,32,512]{2,1,3,0:T(4,128)} %maximum_bitcast_fusion.1) | data formatting | bytes 6291456 | tf_op jit(solution)/shard_map/reshape.57
  643.2 13.9 %all-to-all-done.1 = bf16[8,1,1,3,8192]{4,3,2,1,0:T(4,128)(2,1)S(1)} async-done(((bf16[8,1,1,3,8192]{4,3,2,1,0:T(4,128)(2,1)}), bf16[8,1,1,3,8192]{4,3,2,1,0:T(4,128)(2,1)S(1)}, u32[]{:S(2)}, u32[]{:S(2)}) %all-to-all-start.1) | async-done | bytes 393248 | tf_op jit(solution)/shard_map/all_to_all | solution.py:150
  (119 shorter events, 60.2 us)
Async XLA Ops:
  8.5 27.6 %copy-start.22 = (s32[16]{0:T(128)S(1)}, s32[16]{0:T(128)}, u32[]{:S(2)}) copy-start(s32[16]{0:T(128)} %param.13) | copy-start | bytes 196
  12.4 21.7 %all-to-all-start = ((bf16[8,1,1,3,8192]{4,3,2,1,0:T(4,128)(2,1)}), bf16[8,1,1,3,8192]{4,3,2,1,0:T(4,128)(2,1)S(1)}, u32[]{:S(2)}, u32[]{:S(2)}) async-start(bf16[8,1,1,3,8192]{4,3,2,1,0:T(4,128)(2,1)} %fusion.46), calls=%async_computation | async-start | bytes 1048576 | tf_op jit(solution)/shard_map/all_to_all | solution.py:54
  18.7 233.2 %all-reduce.5.cloned.1.call-start = ((), (), s32[]{:S(2)}) async-start(), calls=%async_computation.2 | async-start | bytes 294912 | tf_op jit(solution)/shard_map/psum | solution.py:105
  18.9 19.3 %copy-start.17 = (f32[256]{0:T(256)}, f32[256]{0:T(256)S(1)}, u32[]{:S(2)}) copy-start(f32[256]{0:T(256)S(1)} %broadcast_subtract_fusion) | copy-start | bytes 3076
  18.9 19.3 %copy-start.19 = (f32[256]{0:T(256)}, f32[256]{0:T(256)S(1)}, u32[]{:S(2)}) copy-start(f32[256]{0:T(256)S(1)} %fusion.138) | copy-start | bytes 3076
  41.2 7.6 %copy-start.21 = (s32[16]{0:T(128)S(1)}, s32[16]{0:T(128)}, u32[]{:S(2)}) copy-start(s32[16]{0:T(128)} %param.12) | copy-start | bytes 196
  70.7 30.7 %copy-start = (f32[16,3,32,256]{2,1,3,0:T(4,128)S(1)}, f32[16,3,32,256]{2,1,3,0:T(4,128)}, u32[]{:S(2)}) copy-start(f32[16,3,32,256]{2,1,3,0:T(4,128)} %copy.155) | copy-start | bytes 4718596
  70.7 30.7 %copy-start.1 = (f32[16,3,32,256]{2,1,3,0:T(4,128)S(1)}, f32[16,3,32,256]{2,1,3,0:T(4,128)}, u32[]{:S(2)}) copy-start(f32[16,3,32,256]{2,1,3,0:T(4,128)} %copy.156) | copy-start | bytes 4718596
  204.6 5.0 copy-start.7
  204.6 5.0 copy-start.9
  204.6 47.3 %copy-start.16 = (f32[16,3,3,256]{3,0,2,1:T(8,128)S(1)}, f32[16,3,3,256]{3,0,2,1:T(8,128)}, u32[]{:S(2)}) copy-start(f32[16,3,3,256]{3,0,2,1:T(8,128)} %param.8) | copy-start | bytes 442372
  204.6 48.6 %copy-start.18 = (f32[256]{0:T(256)S(1)}, f32[256]{0:T(256)}, u32[]{:S(2)}) copy-start(f32[256]{0:T(256)} %copy-done.17) | copy-start | bytes 3076
  204.6 48.6 %copy-start.20 = (f32[256]{0:T(256)S(1)}, f32[256]{0:T(256)}, u32[]{:S(2)}) copy-start(f32[256]{0:T(256)} %copy-done.19) | copy-start | bytes 3076
  258.2 37.4 %copy-start.3 = (f32[16,3,3,256]{1,2,3,0:T(4,128)S(1)}, f32[16,3,3,256]{1,2,3,0:T(4,128)}, u32[]{:S(2)}) copy-start(f32[16,3,3,256]{1,2,3,0:T(4,128)} %copy.174) | copy-start | bytes 442372
  372.1 31.0 %copy-start.2 = (f32[16,3,3,256]{1,2,3,0:T(4,128)S(1)}, f32[16,3,3,256]{1,2,3,0:T(4,128)}, u32[]{:S(2)}) copy-start(f32[16,3,3,256]{1,2,3,0:T(4,128)} %copy.180) | copy-start | bytes 442372
  372.1 61.8 %slice-start.2 = ((s8[8388608]{0:T(1024)(128)(4,1)}), s8[4194304]{0:T(1024)(128)(4,1)S(1)}, s32[]{:S(2)}) async-start(s8[8388608]{0:T(1024)(128)(4,1)} %bitcast.168), calls=%async_computation.5 | async-start | bytes 8388608
  403.1 30.8 %slice-start.3 = ((s8[8388608]{0:T(1024)(128)(4,1)}), s8[4194304]{0:T(1024)(128)(4,1)S(1)}, s32[]{:S(2)}) async-start(s8[8388608]{0:T(1024)(128)(4,1)} %bitcast.168), calls=%async_computation.6 | async-start | bytes 8388608
  403.1 67.5 %slice-start = ((s8[8388608]{0:T(1024)(128)(4,1)}), s8[4194304]{0:T(1024)(128)(4,1)S(1)}, s32[]{:S(2)}) async-start(s8[8388608]{0:T(1024)(128)(4,1)} %bitcast.166), calls=%async_computation.3 | async-start | bytes 8388608
  403.1 67.5 %slice-start.4 = ((s8[8388608]{0:T(1024)(128)(4,1)}), s8[4194304]{0:T(1024)(128)(4,1)S(1)}, s32[]{:S(2)}) async-start(s8[8388608]{0:T(1024)(128)(4,1)} %bitcast.170), calls=%async_computation.7 | async-start | bytes 8388608
  433.9 36.6 %slice-start.1 = ((s8[8388608]{0:T(1024)(128)(4,1)}), s8[4194304]{0:T(1024)(128)(4,1)S(1)}, s32[]{:S(2)}) async-start(s8[8388608]{0:T(1024)(128)(4,1)} %bitcast.166), calls=%async_computation.4 | async-start | bytes 8388608
  433.9 36.6 %slice-start.5 = ((s8[8388608]{0:T(1024)(128)(4,1)}), s8[4194304]{0:T(1024)(128)(4,1)S(1)}, s32[]{:S(2)}) async-start(s8[8388608]{0:T(1024)(128)(4,1)} %bitcast.170), calls=%async_computation.8 | async-start | bytes 8388608
  470.6 36.0 %copy-start.5 = (f32[16,1,3,32,256]{3,2,4,0,1:T(4,128)S(1)}, f32[16,1,3,32,256]{3,2,4,0,1:T(4,128)}, u32[]{:S(2)}) copy-start(f32[16,1,3,32,256]{3,2,4,0,1:T(4,128)} %subtract_bitcast_fusion.1) | copy-start | bytes 4718596
  518.5 11.4 %copy-start.8 = (f32[256,256]{1,0:T(8,128)S(1)}, f32[256,256]{1,0:T(8,128)}, u32[]{:S(2)}) copy-start(f32[256,256]{1,0:T(8,128)} %get-tuple-element.19) | copy-start | bytes 786436
  538.6 31.8 %copy-start.4 = (f32[16,3,3,256]{1,2,3,0:T(4,128)S(1)}, f32[16,3,3,256]{1,2,3,0:T(4,128)}, u32[]{:S(2)}) copy-start(f32[16,3,3,256]{1,2,3,0:T(4,128)} %copy.182) | copy-start | bytes 442372
  617.2 9.8 %copy-start.23 = (s32[16]{0:T(128)S(1)}, s32[16]{0:T(128)}, u32[]{:S(2)}) copy-start(s32[16]{0:T(128)} %param.13) | copy-start | bytes 196
  617.2 11.1 %copy-start.14 = (f32[256,256]{1,0:T(8,128)S(1)}, f32[256,256]{1,0:T(8,128)}, u32[]{:S(2)}) copy-start(f32[256,256]{1,0:T(8,128)} %get-tuple-element.17) | copy-start | bytes 786436
  617.2 11.1 %copy-start.25 = (f32[256]{0:T(256)S(1)}, f32[256]{0:T(256)}, u32[]{:S(2)}) copy-start(f32[256]{0:T(256)} %compare_convert_fusion) | copy-start | bytes 3076
  627.0 6.7 %copy-start.6 = (f32[8,3,32,256]{3,2,1,0:T(8,128)S(1)}, f32[8,3,32,256]{3,2,1,0:T(8,128)}, u32[]{:S(2)}) copy-start(f32[8,3,32,256]{3,2,1,0:T(8,128)} %fusion.3) | copy-start | bytes 2359300
  627.1 6.7 %copy-start.10 = (f32[256,256]{1,0:T(8,128)S(1)}, f32[256,256]{1,0:T(8,128)}, u32[]{:S(2)}) copy-start(f32[256,256]{1,0:T(8,128)} %get-tuple-element.13) | copy-start | bytes 786436
  627.1 6.7 %copy-start.11 = (f32[256,256]{1,0:T(8,128)S(1)}, f32[256,256]{1,0:T(8,128)}, u32[]{:S(2)}) copy-start(f32[256,256]{1,0:T(8,128)} %get-tuple-element.14) | copy-start | bytes 786436
  627.1 29.9 %copy-start.26 = (s32[1,8,1]{1,2,0:T(1,128)S(1)}, s32[1,8,1]{1,2,0:T(1,128)}, u32[]{:S(2)}) copy-start(s32[1,8,1]{1,2,0:T(1,128)} %param.11) | copy-start | bytes 100
  637.0 20.0 %all-to-all-start.1 = ((bf16[8,1,1,3,8192]{4,3,2,1,0:T(4,128)(2,1)}), bf16[8,1,1,3,8192]{4,3,2,1,0:T(4,128)(2,1)S(1)}, u32[]{:S(2)}, u32[]{:S(2)}) async-start(bf16[8,1,1,3,8192]{4,3,2,1,0:T(4,128)(2,1)} %bitcast.61), calls=%async_computation.1 | async-start | bytes 1048576 | tf_op jit(solution)/shard_map/all_to_all | solution.py:150
  (4 other events, 14.2 us)
Sparse Core Ops, SparseCore 0:
  210.9 41.0 all-reduce.4
where the time goes:
time: 670 us; the launch traced here: 666 us
  matrix products  444 us (66%)
  local copies, waits for them, and re-layouts  96.7 us (14%)
  waiting for transfers between devices  56.3 us (8%)
  other arithmetic  42.8 us (6%)
  between operations  15.1 us (2%)
  starting transfers between devices  11 us (2%)
    dot_general x5, matrix products, second_terms(): return jnp.einsum('pwakf,pabf->pwbkf', data, source, precision=highest)  156 us
    dot_general x4, matrix products, first_terms(): return jnp.einsum('pabf,pwbkf->pwakf', source, data, precision=highest)  142 us
    dot_general x4, matrix products, cross_terms(): return jnp.einsum('pwakf,pwbkf->pabf', left, right, precision=highest)  123 us
    another operation x11, local copies, waits for them, and re-layouts  57.7 us
    psum x1, waiting for transfers between devices, shards(): summed = lax.psum(partial_corr, 'win')  35.3 us
    another operation x4, other arithmetic  30.2 us
    all_to_all x1, waiting for transfers between devices, shards(): lax.all_to_all(slot_adjoint, 'stn', split_axis=0, concat_axis=0, tiled=True)  13.9 us
  transfers between devices with their start and end apart: 3, of which 3 were waited for; matrix products, arithmetic and copies ran while one was open for 2% of the time, Pallas kernels for 0%

commit v1 on v0

--- a/solution.py
+++ b/solution.py
@@ -102,7 +102,7 @@
     lag_mask = (lag_ids[None, :] >= lag_lo[:, None]) & (lag_ids[None, :] < lag_hi[:, None])
     share_rows = pair_count // window_groups
     offset = lax.axis_index("win") * share_rows
-    summed = lax.psum(partial_corr, "win")
+    summed = jnp.sum(lax.all_gather(partial_corr, "win"), axis=0)
     residual_all = jnp.where(lag_mask[:, None, None, :], summed * corr_scale - observed, 0.0)
     adjoint_source = residual_all.astype(jnp.bfloat16)
     residual_share = lax.dynamic_slice_in_dim(residual_all, offset, share_rows, 0)

time: 670 us -> 634 us (0.946)
  waiting for transfers between devices: 56.3 us -> 19.9 us
  between operations: 15.1 us -> 1.73 us
  blocking collectives: 0 us -> 10.3 us
    psum x1 -> x0, waiting for transfers between devices: 35.3 us -> none  [shards(): summed = lax.psum(partial_corr, 'win')]
    all_gather x0 -> x1, blocking collectives: none -> 10.3 us  [shards(): summed = jnp.sum(lax.all_gather(partial_corr, 'win'), axis=0)]
  transfers between devices with their start and end apart: 3 -> 2, of which waited for: 3 -> 2; matrix products, arithmetic and copies ran while one was open for 2% -> 2% of each run, Pallas kernels for 0% -> 0%
where the time goes in v1:
time: 634 us; the launch traced here: 624 us
  matrix products  443 us (70%)
  local copies, waits for them, and re-layouts  97.7 us (15%)
  other arithmetic  41.7 us (7%)
  waiting for transfers between devices  19.9 us (3%)
  blocking collectives  10.3 us (2%)
  starting transfers between devices  9.82 us (2%)
    dot_general x5, matrix products, second_terms(): return jnp.einsum('pwakf,pabf->pwbkf', data, source, precision=highest)  156 us
    dot_general x4, matrix products, first_terms(): return jnp.einsum('pabf,pwbkf->pwakf', source, data, precision=highest)  142 us
    dot_general x4, matrix products, cross_terms(): return jnp.einsum('pwakf,pwbkf->pabf', left, right, precision=highest)  123 us
    another operation x11, local copies, waits for them, and re-layouts  58 us
    another operation x4, other arithmetic  30.1 us
    all_to_all x1, waiting for transfers between devices, shards(): lax.all_to_all(slot_adjoint, 'stn', split_axis=0, concat_axis=0, tiled=True)  13.8 us
  transfers between devices with their start and end apart: 2, of which 2 were waited for; matrix products, arithmetic and copies ran while one was open for 2% of the time, Pallas kernels for 0%

profile of v1, /device:TPU:0, one launch (start us, length us, event | category | flops | bytes accessed | tf_op | source)
XLA Modules:
  0.0 623.9 jit_solution(2103884950038483247)
XLA Ops:
  5.9 6.3 %all-to-all-start = ((bf16[8,1,1,3,8192]{4,3,2,1,0:T(4,128)(2,1)}), bf16[8,1,1,3,8192]{4,3,2,1,0:T(4,128)(2,1)S(1)}, u32[]{:S(2)}, u32[]{:S(2)}) async-start(bf16[8,1,1,3,8192]{4,3,2,1,0:T(4,128)(2,1)} %fusion.46), calls=%async_computation | async-start | bytes 1048576 | tf_op jit(solution)/shard_map/all_to_all | solution.py:54
  15.2 6.1 cosine_multiply_fusion.2
  21.4 6.2 all-to-all-done
  34.6 6.2 copy.158
  45.8 6.2 copy.157
  52.0 6.3 %copy.156 = f32[16,3,32,256]{2,1,3,0:T(4,128)} copy(f32[16,3,32,256]{3,0,2,1:T(8,128)} %get-tuple-element.2) | data formatting | bytes 3145728 | tf_op jit(solution)/shard_map/reshape.27
  58.2 6.1 copy.155
  64.4 30.4 %fusion.150 = f32[16,256,3,3]{3,2,1,0:T(4,128)S(1)} fusion(f32[16,3,32,256]{2,1,3,0:T(4,128)} %copy.158, f32[16,3,32,256]{2,1,3,0:T(4,128)} %copy.157), kind=kOutput, calls=%fused_computation.225 | convolution fusion | flops 14155776 | bytes 3293184 | tf_op jit(solution)/shard_map/pwakf,pwbkf->pabf/dot_general | solution.py:94
  94.8 29.9 %subtract_bitcast_fusion.2 = f32[16,3,3,256]{1,2,3,0:T(4,128)} fusion(f32[16,256,3,3]{3,2,1,0:T(4,128)S(1)} %fusion.150, f32[16,3,32,256]{2,1,3,0:T(4,128)S(1)} %copy-done.1, f32[16,3,32,256]{2,1,3,0:T(4,128)S(1)} %copy-done), kind=kOutput, calls=%fused_computation.9 | convolution fusion | flops 14192640 | bytes 3440640 | tf_op jit(solution)/shard_map/pwakf,pwbkf->pabf/dot_general | solution.py:94
  124.7 4.9 copy.163
  129.6 6.1 copy.164
  135.7 30.4 %fusion.149 = f32[16,256,3,3]{3,2,1,0:T(4,128)S(1)} fusion(f32[16,3,32,256]{2,1,3,0:T(4,128)} %copy.164, f32[16,3,32,256]{2,1,3,0:T(4,128)} %copy.155), kind=kOutput, calls=%fused_computation.224 | convolution fusion | flops 14155776 | bytes 3293184 | tf_op jit(solution)/shard_map/pwakf,pwbkf->pabf/dot_general | solution.py:94
  166.2 31.9 %add_bitcast_fusion.2 = f32[16,3,3,256]{1,2,3,0:T(4,128)} fusion(f32[16,256,3,3]{3,2,1,0:T(4,128)S(1)} %fusion.149, f32[16,3,32,256]{2,1,3,0:T(4,128)} %copy.156, f32[16,3,32,256]{2,1,3,0:T(4,128)} %copy.157), kind=kOutput, calls=%fused_computation.10 | convolution fusion | flops 14192640 | bytes 3440640 | tf_op jit(solution)/shard_map/pwakf,pwbkf->pabf/dot_general | solution.py:94
  198.1 5.0 copy.162
  203.5 10.3 %all-gather = f32[64,3,3,256]{3,0,2,1:T(8,128)S(1)} all-gather(f32[16,3,3,256]{3,0,2,1:T(8,128)S(1)} %fusion.47), channel_id=2, replica_groups=mesh['stn'=8,'win'=4] {'win'}, dimensions={0}, use_global_device_ids=true | all-gather | bytes 737280 | tf_op jit(solution)/shard_map/all_gather | solution.py:105
  214.6 5.1 copy.174
  219.7 37.0 %fusion.151 = f32[16,256,32,3]{2,3,1,0:T(4,128)} fusion(f32[16,3,32,256]{2,1,3,0:T(4,128)} %copy.164, f32[16,3,3,256]{1,2,3,0:T(4,128)} %copy.174), kind=kOutput, calls=%fused_computation.226 | convolution fusion | flops 14155776 | bytes 3293184 | tf_op jit(solution)/shard_map/pabf,pwbkf->pwakf/dot_general | solution.py:117
  256.7 30.2 %fusion.153 = f32[16,256,3,32]{3,2,1,0:T(4,128)} fusion(f32[16,3,3,256]{1,2,3,0:T(4,128)S(1)} %copy-done.3, f32[16,3,32,256]{2,1,3,0:T(4,128)} %copy.155), kind=kOutput, calls=%fused_computation.228 | convolution fusion | flops 14155776 | bytes 3293184 | tf_op jit(solution)/shard_map/pwakf,pabf->pwbkf/dot_general | solution.py:125
  286.9 4.8 copy.169
  291.7 32.2 %fusion.152 = f32[16,256,32,3]{2,3,1,0:T(4,128)} fusion(f32[16,3,32,256]{2,1,3,0:T(4,128)} %copy.158, f32[16,3,3,256]{2,1,3,0:T(4,128)} %copy.169), kind=kOutput, calls=%fused_computation.227 | convolution fusion | flops 14155776 | bytes 3293184 | tf_op jit(solution)/shard_map/pabf,pwbkf->pwakf/dot_general | solution.py:117
  323.9 4.8 copy.166
  338.0 31.0 %fusion.154 = f32[16,256,3,32]{3,2,1,0:T(4,128)} fusion(f32[16,3,3,256]{1,2,3,0:T(4,128)} %copy.176, f32[16,3,32,256]{2,1,3,0:T(4,128)} %copy.155), kind=kOutput, calls=%fused_computation.229 | convolution fusion | flops 14155776 | bytes 3293184 | tf_op jit(solution)/shard_map/pwakf,pabf->pwbkf/dot_general | solution.py:125
  369.0 30.8 %fusion.155 = f32[16,256,3,32]{3,2,1,0:T(4,128)} fusion(f32[16,3,3,256]{1,2,3,0:T(4,128)S(1)} %copy-done.2, f32[16,3,32,256]{2,1,3,0:T(4,128)} %copy.157), kind=kOutput, calls=%fused_computation.230 | convolution fusion | flops 14155776 | bytes 3293184 | tf_op jit(solution)/shard_map/pwakf,pabf->pwbkf/dot_general | solution.py:125
  399.9 36.7 %subtract_bitcast_fusion.1 = f32[16,1,3,32,256]{3,2,4,0,1:T(4,128)} fusion(f32[16,256,32,3]{2,3,1,0:T(4,128)} %fusion.152, f32[16,3,32,256]{2,1,3,0:T(4,128)S(1)} %bitcast.170, f32[16,3,3,256]{1,2,3,0:T(4,128)S(1)} %copy-done.2), kind=kOutput, calls=%fused_computation.7 | convolution fusion | flops 14548992 | bytes 4866048 | tf_op jit(solution)/shard_map/pabf,pwbkf->pwakf/dot_general | solution.py:117
  436.6 36.0 %add_bitcast_fusion.1 = f32[16,1,3,32,256]{3,2,4,0,1:T(4,128)} fusion(f32[16,256,32,3]{2,3,1,0:T(4,128)S(1)} %bitcast.172, f32[16,3,32,256]{2,1,3,0:T(4,128)S(1)} %bitcast.170, f32[16,3,3,256]{1,2,3,0:T(4,128)S(1)} %bitcast.168), kind=kOutput, calls=%fused_computation.8 | convolution fusion | flops 14548992 | bytes 4866048 | tf_op jit(solution)/shard_map/pabf,pwbkf->pwakf/dot_general | solution.py:117
  472.6 11.9 %maximum_bitcast_fusion = f32[16,3,32,512]{2,1,3,0:T(4,128)} fusion(f32[16,1,3,32,256]{3,2,4,0,1:T(4,128)S(1)} %copy-done.5, f32[16,1,3,32,256]{3,2,4,0,1:T(4,128)} %add_bitcast_fusion.1), kind=kLoop, calls=%fused_computation.1 | loop fusion | flops 786432 | bytes 6291456 | tf_op jit(solution)/shard_map/reshape.43
  484.5 9.5 %copy.172 = f32[16,3,32,512]{3,0,2,1:T(8,128)S(1)} copy(f32[16,3,32,512]{2,1,3,0:T(4,128)} %maximum_bitcast_fusion) | data formatting | bytes 6291456 | tf_op jit(solution)/shard_map/reshape.43
  504.6 31.8 %subtract_bitcast_fusion = f32[16,1,3,32,256]{3,2,4,0,1:T(4,128)} fusion(f32[16,256,3,32]{3,2,1,0:T(4,128)} %fusion.153, f32[16,3,3,256]{1,2,3,0:T(4,128)} %copy.176, f32[16,3,32,256]{2,1,3,0:T(4,128)} %copy.157), kind=kOutput, calls=%fused_computation.6 | convolution fusion | flops 14548992 | bytes 4866048 | tf_op jit(solution)/shard_map/pwakf,pabf->pwbkf/dot_general | solution.py:125
  536.4 31.8 %add_bitcast_fusion = f32[16,1,3,32,256]{3,2,4,0,1:T(4,128)} fusion(f32[16,256,3,32]{3,2,1,0:T(4,128)} %fusion.154, f32[16,256,3,32]{3,2,1,0:T(4,128)} %fusion.155, f32[16,3,3,256]{1,2,3,0:T(4,128)S(1)} %copy-done.4, f32[16,3,32,256]{2,1,3,0:T(4,128)} %copy.157), kind=kOutput, calls=%fused_computation.5 | convolution fusion | flops 14942208 | bytes 6438912 | tf_op jit(solution)/shard_map/pwakf,pabf->pwbkf/dot_general | solution.py:125
  568.3 15.0 %maximum_bitcast_fusion.1 = f32[16,3,32,512]{2,1,3,0:T(4,128)} fusion(f32[16,1,3,32,256]{3,2,4,0,1:T(4,128)} %add_bitcast_fusion, f32[16,1,3,32,256]{3,2,4,0,1:T(4,128)} %subtract_bitcast_fusion), kind=kLoop, calls=%fused_computation.2 | loop fusion | flops 786432 | bytes 6291456 | tf_op jit(solution)/shard_map/reshape.57
  583.2 9.8 %copy.184 = f32[16,3,32,512]{3,0,2,1:T(8,128)S(1)} copy(f32[16,3,32,512]{2,1,3,0:T(4,128)} %maximum_bitcast_fusion.1) | data formatting | bytes 6291456 | tf_op jit(solution)/shard_map/reshape.57
  608.1 13.8 %all-to-all-done.1 = bf16[8,1,1,3,8192]{4,3,2,1,0:T(4,128)(2,1)S(1)} async-done(((bf16[8,1,1,3,8192]{4,3,2,1,0:T(4,128)(2,1)}), bf16[8,1,1,3,8192]{4,3,2,1,0:T(4,128)(2,1)S(1)}, u32[]{:S(2)}, u32[]{:S(2)}) %all-to-all-start.1) | async-done | bytes 393248 | tf_op jit(solution)/shard_map/all_to_all | solution.py:150
  (118 shorter events, 57.7 us)
Async XLA Ops:
  2.0 27.6 %copy-start.22 = (s32[16]{0:T(128)S(1)}, s32[16]{0:T(128)}, u32[]{:S(2)}) copy-start(s32[16]{0:T(128)} %param.13) | copy-start | bytes 196
  5.9 21.7 %all-to-all-start = ((bf16[8,1,1,3,8192]{4,3,2,1,0:T(4,128)(2,1)}), bf16[8,1,1,3,8192]{4,3,2,1,0:T(4,128)(2,1)S(1)}, u32[]{:S(2)}, u32[]{:S(2)}) async-start(bf16[8,1,1,3,8192]{4,3,2,1,0:T(4,128)(2,1)} %fusion.46), calls=%async_computation | async-start | bytes 1048576 | tf_op jit(solution)/shard_map/all_to_all | solution.py:54
  12.3 19.4 %copy-start.17 = (f32[256]{0:T(256)}, f32[256]{0:T(256)S(1)}, u32[]{:S(2)}) copy-start(f32[256]{0:T(256)S(1)} %broadcast_subtract_fusion) | copy-start | bytes 3076
  12.3 19.4 %copy-start.19 = (f32[256]{0:T(256)}, f32[256]{0:T(256)S(1)}, u32[]{:S(2)}) copy-start(f32[256]{0:T(256)S(1)} %fusion.138) | copy-start | bytes 3076
  34.6 7.6 %copy-start.21 = (s32[16]{0:T(128)S(1)}, s32[16]{0:T(128)}, u32[]{:S(2)}) copy-start(s32[16]{0:T(128)} %param.12) | copy-start | bytes 196
  64.4 30.5 %copy-start = (f32[16,3,32,256]{2,1,3,0:T(4,128)S(1)}, f32[16,3,32,256]{2,1,3,0:T(4,128)}, u32[]{:S(2)}) copy-start(f32[16,3,32,256]{2,1,3,0:T(4,128)} %copy.155) | copy-start | bytes 4718596
  64.4 30.5 %copy-start.1 = (f32[16,3,32,256]{2,1,3,0:T(4,128)S(1)}, f32[16,3,32,256]{2,1,3,0:T(4,128)}, u32[]{:S(2)}) copy-start(f32[16,3,32,256]{2,1,3,0:T(4,128)} %copy.156) | copy-start | bytes 4718596
  198.1 5.0 copy-start.7
  198.1 5.0 copy-start.9
  198.1 15.8 %copy-start.16 = (f32[16,3,3,256]{3,0,2,1:T(8,128)S(1)}, f32[16,3,3,256]{3,0,2,1:T(8,128)}, u32[]{:S(2)}) copy-start(f32[16,3,3,256]{3,0,2,1:T(8,128)} %param.8) | copy-start | bytes 442372
  198.1 16.2 %copy-start.18 = (f32[256]{0:T(256)S(1)}, f32[256]{0:T(256)}, u32[]{:S(2)}) copy-start(f32[256]{0:T(256)} %copy-done.17) | copy-start | bytes 3076
  198.1 16.2 %copy-start.20 = (f32[256]{0:T(256)S(1)}, f32[256]{0:T(256)}, u32[]{:S(2)}) copy-start(f32[256]{0:T(256)} %copy-done.19) | copy-start | bytes 3076
  219.7 37.0 %copy-start.3 = (f32[16,3,3,256]{1,2,3,0:T(4,128)S(1)}, f32[16,3,3,256]{1,2,3,0:T(4,128)}, u32[]{:S(2)}) copy-start(f32[16,3,3,256]{1,2,3,0:T(4,128)} %copy.174) | copy-start | bytes 442372
  338.0 31.0 %copy-start.2 = (f32[16,3,3,256]{1,2,3,0:T(4,128)S(1)}, f32[16,3,3,256]{1,2,3,0:T(4,128)}, u32[]{:S(2)}) copy-start(f32[16,3,3,256]{1,2,3,0:T(4,128)} %copy.180) | copy-start | bytes 442372
  338.0 61.9 %slice-start.2 = ((s8[8388608]{0:T(1024)(128)(4,1)}), s8[4194304]{0:T(1024)(128)(4,1)S(1)}, s32[]{:S(2)}) async-start(s8[8388608]{0:T(1024)(128)(4,1)} %bitcast.169), calls=%async_computation.4 | async-start | bytes 8388608
  369.0 30.9 %slice-start.3 = ((s8[8388608]{0:T(1024)(128)(4,1)}), s8[4194304]{0:T(1024)(128)(4,1)S(1)}, s32[]{:S(2)}) async-start(s8[8388608]{0:T(1024)(128)(4,1)} %bitcast.169), calls=%async_computation.5 | async-start | bytes 8388608
  369.0 67.5 %slice-start = ((s8[8388608]{0:T(1024)(128)(4,1)}), s8[4194304]{0:T(1024)(128)(4,1)S(1)}, s32[]{:S(2)}) async-start(s8[8388608]{0:T(1024)(128)(4,1)} %bitcast.167), calls=%async_computation.2 | async-start | bytes 8388608
  369.0 67.5 %slice-start.4 = ((s8[8388608]{0:T(1024)(128)(4,1)}), s8[4194304]{0:T(1024)(128)(4,1)S(1)}, s32[]{:S(2)}) async-start(s8[8388608]{0:T(1024)(128)(4,1)} %bitcast.171), calls=%async_computation.6 | async-start | bytes 8388608
  399.9 36.7 %slice-start.1 = ((s8[8388608]{0:T(1024)(128)(4,1)}), s8[4194304]{0:T(1024)(128)(4,1)S(1)}, s32[]{:S(2)}) async-start(s8[8388608]{0:T(1024)(128)(4,1)} %bitcast.167), calls=%async_computation.3 | async-start | bytes 8388608
  399.9 36.7 %slice-start.5 = ((s8[8388608]{0:T(1024)(128)(4,1)}), s8[4194304]{0:T(1024)(128)(4,1)S(1)}, s32[]{:S(2)}) async-start(s8[8388608]{0:T(1024)(128)(4,1)} %bitcast.171), calls=%async_computation.7 | async-start | bytes 8388608
  436.6 36.0 %copy-start.5 = (f32[16,1,3,32,256]{3,2,4,0,1:T(4,128)S(1)}, f32[16,1,3,32,256]{3,2,4,0,1:T(4,128)}, u32[]{:S(2)}) copy-start(f32[16,1,3,32,256]{3,2,4,0,1:T(4,128)} %subtract_bitcast_fusion.1) | copy-start | bytes 4718596
  484.5 11.4 %copy-start.8 = (f32[256,256]{1,0:T(8,128)S(1)}, f32[256,256]{1,0:T(8,128)}, u32[]{:S(2)}) copy-start(f32[256,256]{1,0:T(8,128)} %get-tuple-element.19) | copy-start | bytes 786436
  504.6 31.8 %copy-start.4 = (f32[16,3,3,256]{1,2,3,0:T(4,128)S(1)}, f32[16,3,3,256]{1,2,3,0:T(4,128)}, u32[]{:S(2)}) copy-start(f32[16,3,3,256]{1,2,3,0:T(4,128)} %copy.182) | copy-start | bytes 442372
  583.2 9.8 %copy-start.23 = (s32[16]{0:T(128)S(1)}, s32[16]{0:T(128)}, u32[]{:S(2)}) copy-start(s32[16]{0:T(128)} %param.13) | copy-start | bytes 196
  583.2 11.1 %copy-start.14 = (f32[256,256]{1,0:T(8,128)S(1)}, f32[256,256]{1,0:T(8,128)}, u32[]{:S(2)}) copy-start(f32[256,256]{1,0:T(8,128)} %get-tuple-element.17) | copy-start | bytes 786436
  583.2 11.1 %copy-start.25 = (f32[256]{0:T(256)S(1)}, f32[256]{0:T(256)}, u32[]{:S(2)}) copy-start(f32[256]{0:T(256)} %compare_convert_fusion) | copy-start | bytes 3076
  593.0 4.5 copy-start.12
  593.0 6.7 %copy-start.6 = (f32[8,3,32,256]{3,2,1,0:T(8,128)S(1)}, f32[8,3,32,256]{3,2,1,0:T(8,128)}, u32[]{:S(2)}) copy-start(f32[8,3,32,256]{3,2,1,0:T(8,128)} %fusion.3) | copy-start | bytes 2359300
  593.0 6.7 %copy-start.10 = (f32[256,256]{1,0:T(8,128)S(1)}, f32[256,256]{1,0:T(8,128)}, u32[]{:S(2)}) copy-start(f32[256,256]{1,0:T(8,128)} %get-tuple-element.13) | copy-start | bytes 786436
  593.1 6.7 %copy-start.11 = (f32[256,256]{1,0:T(8,128)S(1)}, f32[256,256]{1,0:T(8,128)}, u32[]{:S(2)}) copy-start(f32[256,256]{1,0:T(8,128)} %get-tuple-element.14) | copy-start | bytes 786436
  593.1 28.8 %copy-start.26 = (s32[1,8,1]{1,2,0:T(1,128)S(1)}, s32[1,8,1]{1,2,0:T(1,128)}, u32[]{:S(2)}) copy-start(s32[1,8,1]{1,2,0:T(1,128)} %param.11) | copy-start | bytes 100
  603.0 18.8 %all-to-all-start.1 = ((bf16[8,1,1,3,8192]{4,3,2,1,0:T(4,128)(2,1)}), bf16[8,1,1,3,8192]{4,3,2,1,0:T(4,128)(2,1)S(1)}, u32[]{:S(2)}, u32[]{:S(2)}) async-start(bf16[8,1,1,3,8192]{4,3,2,1,0:T(4,128)(2,1)} %bitcast.62), calls=%async_computation.1 | async-start | bytes 1048576 | tf_op jit(solution)/shard_map/all_to_all | solution.py:150
  (3 other events, 9.7 us)
